TPU v7x, 32 devices: a whole 2x2x4 slice. The times are simulated.
32 devices in a mesh: dp: 4 (over y, x), expert: 8 (over z, core).
Axes of the slice: x: 2, y: 2, z: 4, core: 2. Of those that a mesh axis runs over, the one named last changes fastest.
Arguments:
- tokens: bfloat16 [4096, 1536], P(('dp', 'expert')), may hold values from -6 to 6
- grad_out: bfloat16 [4096, 1536], P(('dp', 'expert')), may hold values from -6 to 6
- expert_ids: int32 [4096, 4], P(('dp', 'expert')), may hold values from 0 to 7, all different within a row; in each aligned block of 128 rows (0 to 127, 128 to 255, ...) at most 96 rows name the same one
- gate_q: int32 [4096, 4], P(('dp', 'expert')), may hold values from 1 to 65535
- w_up: bfloat16 [8, 1536, 768], P('expert', 'dp'), may hold values from -0.15625 to 0.15625
- w_down: bfloat16 [8, 768, 1536], P('expert', None, 'dp'), may hold values from -0.21875 to 0.21875
Outputs:
- dw_up: bfloat16 [8, 1536, 768], P('expert', 'dp')
- dw_down: bfloat16 [8, 768, 1536], P('expert', None, 'dp')
Inputs may be any that keep to these rules, and one draw needn't show every extreme that they name: `expert_ids`: within the rows of one device no expert is named by more than 96 rows, a bound that some block reaches; the 4 ids of a row differ.
All inputs are finite; a program needn't handle non-finite values.
Results may differ from a plain program's by a relative error of at most 0.0064.
Values may be sent and summed in bfloat16 or wider, within the bound.
No kernel may reach another device: no remote copies, remote signals or barrier semaphores. Data moves between devices by JAX's collectives and lax.ppermute only.
A program may use at most 64 MiB of HBM per device.

v0:
```python
import jax
import jax.numpy as jnp
from jax import lax
from jax.sharding import PartitionSpec as P


def silu_slope(values):
    sigmoid_part = jax.nn.sigmoid(values)
    return sigmoid_part * (1.0 + values * (1.0 - sigmoid_part))


def summed_up(recv_rows, projected_grad):
    first_dims = (((0,), (0,)), ((), ()))
    partial_value = lax.dot_general(
        recv_rows, projected_grad, first_dims, preferred_element_type=jnp.float32
    ).astype(jnp.bfloat16)
    pieces = lax.all_to_all(partial_value[None], "dp", split_axis=1, concat_axis=0, tiled=True)
    return jnp.sum(pieces.astype(jnp.float32), axis=0, keepdims=True).astype(jnp.bfloat16)


def summed_down(activated, grad_rows):
    first_dims = (((0,), (0,)), ((), ()))
    partial_value = lax.dot_general(
        activated, grad_rows, first_dims, preferred_element_type=jnp.float32
    ).astype(jnp.bfloat16)
    pieces = lax.all_to_all(partial_value[None], "dp", split_axis=2, concat_axis=0, tiled=True)
    return jnp.sum(pieces.astype(jnp.float32), axis=0, keepdims=True).astype(jnp.bfloat16)


def shards(tokens, grad_out, expert_ids, gate_q, w_up, w_down):
    devices = lax.axis_size("expert")
    token_count, top_count = expert_ids.shape
    model_width = tokens.shape[1]
    capacity = max(2, token_count * top_count * 3 // (2 * devices))
    slot_expert = expert_ids.reshape(-1)
    onehot_table = (slot_expert[:, None] == jnp.arange(devices, dtype=jnp.int32)[None, :]).astype(
        jnp.int32
    )
    earlier = jnp.cumsum(onehot_table, axis=0) - onehot_table
    slot_rank = jnp.sum(earlier * onehot_table, axis=1)
    slot_target = slot_expert * capacity + slot_rank
    gate_values = gate_q.reshape(-1).astype(jnp.float32) * (1.0 / 65536.0)
    token_rows = jnp.repeat(tokens, top_count, axis=0)
    slot_grads = (
        gate_values[:, None] * jnp.repeat(grad_out, top_count, axis=0).astype(jnp.float32)
    ).astype(jnp.bfloat16)
    empty_rows = jnp.zeros((devices * capacity, model_width), jnp.bfloat16)
    send_tokens = empty_rows.at[slot_target].set(token_rows).reshape(devices, capacity, model_width)
    grad_slots = empty_rows.at[slot_target].set(slot_grads).reshape(devices, capacity, model_width)
    contract_last = (((1,), (1,)), ((), ()))
    up_whole = lax.all_gather(w_up, "dp", axis=1, tiled=True)[0]
    down_whole = lax.all_gather(w_down, "dp", axis=2, tiled=True)[0]
    recv_tokens = lax.all_to_all(send_tokens, "expert", split_axis=0, concat_axis=0, tiled=True)
    recv_rows = recv_tokens.reshape(-1, model_width)
    projected = jnp.dot(recv_rows, up_whole, preferred_element_type=jnp.float32)
    recv_grads = lax.all_to_all(grad_slots, "expert", split_axis=0, concat_axis=0, tiled=True)
    activated = jax.nn.silu(projected).astype(jnp.bfloat16)
    grad_rows = recv_grads.reshape(-1, model_width)
    act_grad = lax.dot_general(
        grad_rows, down_whole, contract_last, preferred_element_type=jnp.float32
    )
    projected_grad = (act_grad * silu_slope(projected)).astype(jnp.bfloat16)
    up_grad = summed_up(recv_rows, projected_grad)
    down_grad = summed_down(activated, grad_rows)
    return (up_grad, down_grad)


def solution(mesh):
    in_specs = (
        P(("dp", "expert"), None),
        P(("dp", "expert"), None),
        P(("dp", "expert"), None),
        P(("dp", "expert"), None),
        P("expert", "dp", None),
        P("expert", None, "dp"),
    )
    out_specs = (P("expert", "dp", None), P("expert", None, "dp"))
    return jax.shard_map(shards, mesh=mesh, in_specs=in_specs, out_specs=out_specs, check_vma=False)
```

profile of v0, /device:TPU:0, one launch (start us, length us, event | category | flops | bytes accessed | tf_op | source)
XLA Modules:
  0.0 307.0 jit_solution(6901323254794781142)
XLA Ops:
  7.2 0.8 copy.25
  8.0 0.1 eq.29
  8.1 0.1 eq.25
  8.2 0.7 broadcast_multiply_fusion
  8.9 1.1 reduce-window.6
  10.0 0.2 slice_reduce_fusion
  10.2 0.1 copy.24
  10.4 0.1 mul.55
  10.5 1.4 broadcast_in_dim.22
  11.9 0.4 reshape.112
  12.3 0.1 fusion.17
  12.4 4.7 %scatter_custom_fusion = bf16[768,1536]{1,0:T(8,128)(2,1)} fusion(s32[512]{0:T(512)S(1)} %bitcast.53, bf16[512,1536]{1,0:T(8,128)(2,1)S(1)} %reshape.112, bf16[]{:T(256)} %constant.7.clone.1), kind=kCustom, calls=%fused_computation.18 | custom fusion | bytes 2359298 | tf_op jit(solution)/shard_map/scatter | solution.py:48
  17.1 0.0 copy-start.1
  17.1 6.5 %all-to-all-start = ((bf16[8,96,1536]{2,1,0:T(8,128)(2,1)}), bf16[8,96,1536]{2,1,0:T(8,128)(2,1)}, u32[]{:S(2)}, u32[]{:S(2)}) async-start(bf16[8,96,1536]{2,1,0:T(8,128)(2,1)} %bitcast.4), calls=%async_computation | async-start | bytes 4718592 | tf_op jit(solution)/shard_map/all_to_all | solution.py:53
  23.6 0.0 all-gather.5.cloned.1.call-start
  23.6 0.7 all-gather.5.cloned.1.call-update
  24.3 0.0 copy-done.1
  24.3 0.4 broadcast_in_dim.23
  24.7 0.0 copy-start.2
  24.7 2.3 convert_element_type.78
  27.0 0.0 copy-done.2
  27.0 0.1 copy.27
  27.1 0.1 mul.59
  27.2 6.0 %scatter_custom_fusion.1 = bf16[768,1536]{1,0:T(8,128)(2,1)} fusion(s32[512]{0:T(512)S(1)} %bitcast.54, f32[512,1536]{1,0:T(8,128)} %convert_element_type.78, f32[512]{0:T(512)S(1)} %mul.59, bf16[]{:T(256)} %constant.7.clone.1), kind=kCustom, calls=%fused_computation.14 | custom fusion | flops 1572864 | bytes 5507074 | tf_op jit(solution)/shard_map/scatter | solution.py:49
  33.3 45.1 %all-to-all-done = bf16[8,96,1536]{2,1,0:T(8,128)(2,1)} async-done(((bf16[8,96,1536]{2,1,0:T(8,128)(2,1)}), bf16[8,96,1536]{2,1,0:T(8,128)(2,1)}, u32[]{:S(2)}, u32[]{:S(2)}) %all-to-all-start) | async-done | bytes 2359328 | tf_op jit(solution)/shard_map/all_to_all | solution.py:53
  78.3 3.6 %all-to-all-start.1 = ((bf16[8,96,1536]{2,1,0:T(8,128)(2,1)}), bf16[8,96,1536]{2,1,0:T(8,128)(2,1)S(1)}, u32[]{:S(2)}, u32[]{:S(2)}) async-start(bf16[8,96,1536]{2,1,0:T(8,128)(2,1)} %bitcast.6), calls=%async_computation.1 | async-start | bytes 4718592 | tf_op jit(solution)/shard_map/all_to_all | solution.py:56
  81.9 0.2 all-gather.3.cloned.1.call-start
  82.2 0.5 all-gather.3.cloned.1.call-update
  82.7 0.0 all-gather.5.cloned.1.call-done
  82.7 5.8 %fusion.2 = f32[768,768]{1,0:T(8,128)} fusion(bf16[768,1536]{1,0:T(8,128)(2,1)} %bitcast.5, bf16[1,1536,768]{2,1,0:T(8,128)(2,1)} %all-gather.5.cloned.1.call-done), kind=kOutput, calls=%fused_computation.7 | convolution fusion | flops 1811939328 | bytes 7077888 | tf_op jit(solution)/shard_map/dot_general | solution.py:55
  88.5 34.7 %all-gather.3.cloned.1.call-done = bf16[1,768,1536]{2,1,0:T(8,128)(2,1)} async-done(((bf16[1,768,384]{2,1,0:T(8,128)(2,1)}), bf16[1,768,1536]{2,1,0:T(8,128)(2,1)}) %all-gather.3.cloned.1.call-update) | async-done | bytes 2359312 | tf_op jit(solution)/shard_map/all_gather | solution.py:52
  123.2 13.3 %all-to-all-done.1 = bf16[8,96,1536]{2,1,0:T(8,128)(2,1)S(1)} async-done(((bf16[8,96,1536]{2,1,0:T(8,128)(2,1)}), bf16[8,96,1536]{2,1,0:T(8,128)(2,1)S(1)}, u32[]{:S(2)}, u32[]{:S(2)}) %all-to-all-start.1) | async-done | bytes 2359328 | tf_op jit(solution)/shard_map/all_to_all | solution.py:56
  136.5 0.0 copy-start
  136.5 1.4 copy-done
  137.9 8.2 %fusion = bf16[1,1536,768]{2,1,0:T(8,128)(2,1)S(1)} fusion(bf16[768,1536]{1,0:T(8,128)(2,1)} %bitcast.5, f32[768,768]{1,0:T(8,128)} %fusion.2, bf16[768,1536]{1,0:T(8,128)(2,1)} %bitcast.48, bf16[1,768,1536]{2,1,0:T(8,128)(2,1)} %all-gather.3.cloned.1.call-done), kind=kOutput, calls=%fused_computation.5 | convolution fusion | flops 3630366720 | bytes 11796480 | tf_op jit(solution)/shard_map/dot_general | solution.py:14
  146.1 33.8 %copy.34 = bf16[1,1536,768]{2,0,1:T(2,128)(2,1)} copy(bf16[1,1536,768]{2,1,0:T(8,128)(2,1)S(1)} %fusion) | data formatting | bytes 4718592 | tf_op jit(solution)/shard_map/broadcast_in_dim | solution.py:17
  179.9 0.5 broadcast.72
  180.4 24.1 %reduce.7 = bf16[1536,768]{1,0:T(8,128)(2,1)S(1)} reduce(bf16[1536,1,768]{2,1,0:T(2,128)(2,1)} %bitcast.42, bf16[]{:T(256)} %broadcast.72), dimensions={1}, to_apply=%bitcast.41.reduce_sub_computation | reduce | bytes 4718594
  204.5 2.3 reshape.129
  206.8 3.9 %all-to-all-start.2 = ((bf16[4,2,147456]{2,1,0:T(2,128)(2,1)}), bf16[4,2,147456]{2,1,0:T(2,128)(2,1)S(1)}, u32[]{:S(2)}, u32[]{:S(2)}) async-start(bf16[4,2,147456]{2,1,0:T(2,128)(2,1)} %reshape.129), calls=%async_computation.2 | async-start | bytes 4718592 | tf_op jit(solution)/shard_map/all_to_all | solution.py:17
  210.6 5.9 %fusion.1 = bf16[1,768,1536]{2,1,0:T(8,128)(2,1)} fusion(bf16[768,1536]{1,0:T(8,128)(2,1)} %bitcast.49, f32[768,768]{1,0:T(8,128)} %fusion.2), kind=kOutput, calls=%fused_computation.6 | convolution fusion | flops 1816068096 | bytes 7077888 | tf_op jit(solution)/shard_map/dot_general | solution.py:23
  216.5 12.1 %copy.29 = bf16[1,768,1536]{1,0,2:T(2,128)(2,1)} copy(bf16[1,768,1536]{2,1,0:T(8,128)(2,1)} %fusion.1) | data formatting | bytes 4718592 | tf_op jit(solution)/shard_map/broadcast_in_dim | solution.py:26
  228.6 25.5 %reduce.8 = bf16[1536,768]{1,0:T(8,128)(2,1)} reduce(bf16[1536,1,768]{2,1,0:T(2,128)(2,1)} %bitcast.43, bf16[]{:T(256)} %broadcast.72), dimensions={1}, to_apply=%bitcast.34.reduce_sub_computation | reduce | bytes 4718594
  254.1 4.1 %reshape.131 = bf16[4,2,147456]{2,1,0:T(2,128)(2,1)} reshape(bf16[1536,768]{1,0:T(8,128)(2,1)} %reduce.8) | data formatting | bytes 4718592
  258.2 0.0 all-to-all-done.2
  258.2 4.5 %all-to-all-start.3 = ((bf16[4,2,147456]{2,1,0:T(2,128)(2,1)}), bf16[4,2,147456]{2,1,0:T(2,128)(2,1)}, u32[]{:S(2)}, u32[]{:S(2)}) async-start(bf16[4,2,147456]{2,1,0:T(2,128)(2,1)} %reshape.131), calls=%async_computation.3 | async-start | bytes 4718592 | tf_op jit(solution)/shard_map/all_to_all | solution.py:26
  262.7 3.6 %reshape.130 = bf16[1536,1,768]{2,1,0:T(2,128)(2,1)} reshape(bf16[4,2,147456]{2,1,0:T(2,128)(2,1)S(1)} %all-to-all-done.2) | data formatting | bytes 4718592
  266.3 2.7 copy.31
  269.0 1.3 reduce.4
  270.3 20.1 %all-to-all-done.3 = bf16[4,2,147456]{2,1,0:T(2,128)(2,1)} async-done(((bf16[4,2,147456]{2,1,0:T(2,128)(2,1)}), bf16[4,2,147456]{2,1,0:T(2,128)(2,1)}, u32[]{:S(2)}, u32[]{:S(2)}) %all-to-all-start.3) | async-done | bytes 2359328 | tf_op jit(solution)/shard_map/all_to_all | solution.py:26
  290.5 5.2 %reshape.132 = bf16[1536,1,768]{2,1,0:T(2,128)(2,1)} reshape(bf16[4,2,147456]{2,1,0:T(2,128)(2,1)} %all-to-all-done.3) | data formatting | bytes 4718592
  295.6 2.7 copy.32
  298.4 0.7 reduce_sum.35
  299.1 1.1 copy.30
  (5 shorter events, 0.1 us)
Async XLA Ops:
  17.1 7.2 %copy-start.1 = (bf16[128,1536]{1,0:T(8,128)(2,1)S(1)}, bf16[128,1536]{1,0:T(8,128)(2,1)}, u32[]{:S(2)}) copy-start(bf16[128,1536]{1,0:T(8,128)(2,1)} %param.7) | copy-start | bytes 1179652
  17.1 61.2 %all-to-all-start = ((bf16[8,96,1536]{2,1,0:T(8,128)(2,1)}), bf16[8,96,1536]{2,1,0:T(8,128)(2,1)}, u32[]{:S(2)}, u32[]{:S(2)}) async-start(bf16[8,96,1536]{2,1,0:T(8,128)(2,1)} %bitcast.4), calls=%async_computation | async-start | bytes 4718592 | tf_op jit(solution)/shard_map/all_to_all | solution.py:53
  23.6 59.2 %all-gather.5.cloned.1.call-start = ((), (), s32[]{:S(2)}) async-start(), calls=%async_computation.5 | async-start | bytes 2949120 | tf_op jit(solution)/shard_map/all_gather | solution.py:51
  24.7 2.3 copy-start.2
  78.3 58.2 %all-to-all-start.1 = ((bf16[8,96,1536]{2,1,0:T(8,128)(2,1)}), bf16[8,96,1536]{2,1,0:T(8,128)(2,1)S(1)}, u32[]{:S(2)}, u32[]{:S(2)}) async-start(bf16[8,96,1536]{2,1,0:T(8,128)(2,1)} %bitcast.6), calls=%async_computation.1 | async-start | bytes 4718592 | tf_op jit(solution)/shard_map/all_to_all | solution.py:56
  81.9 41.3 %all-gather.3.cloned.1.call-start = ((), (), s32[]{:S(2)}) async-start(), calls=%async_computation.4 | async-start | bytes 2949120 | tf_op jit(solution)/shard_map/all_gather | solution.py:52
  136.5 1.4 copy-start
  206.8 51.5 %all-to-all-start.2 = ((bf16[4,2,147456]{2,1,0:T(2,128)(2,1)}), bf16[4,2,147456]{2,1,0:T(2,128)(2,1)S(1)}, u32[]{:S(2)}, u32[]{:S(2)}) async-start(bf16[4,2,147456]{2,1,0:T(2,128)(2,1)} %reshape.129), calls=%async_computation.2 | async-start | bytes 4718592 | tf_op jit(solution)/shard_map/all_to_all | solution.py:17
  258.2 32.2 %all-to-all-start.3 = ((bf16[4,2,147456]{2,1,0:T(2,128)(2,1)}), bf16[4,2,147456]{2,1,0:T(2,128)(2,1)}, u32[]{:S(2)}, u32[]{:S(2)}) async-start(bf16[4,2,147456]{2,1,0:T(2,128)(2,1)} %reshape.131), calls=%async_computation.3 | async-start | bytes 4718592 | tf_op jit(solution)/shard_map/all_to_all | solution.py:26
Sparse Core Ops, SparseCore 0:
  26.2 38.7 all-gather.4
  84.6 38.5 all-gather.2
where the time goes:
time: 308 us; the launch traced here: 307 us
  waiting for transfers between devices  114 us (37%)
  local copies, waits for them, and re-layouts  80.2 us (26%)
  other arithmetic  59.7 us (19%)
  matrix products  19.9 us (6%)
  starting transfers between devices  18.7 us (6%)
  between operations  14.2 us (5%)
    unnamed x2, other arithmetic  49.6 us
    all_to_all x1, waiting for transfers between devices, shards(): lax.all_to_all(send_tokens, 'expert', split_axis=0, concat_axis=0, tiled=...  45.1 us
    all_gather x1, waiting for transfers between devices, shards(): down_whole = lax.all_gather(w_down, 'dp', axis=2, tiled=True)[0]  34.7 us
    broadcast_in_dim x1, local copies, waits for them, and re-layouts, summed_up(): partial_value[None]  33.8 us
    unnamed x15, local copies, waits for them, and re-layouts  24.3 us
    all_to_all x1, waiting for transfers between devices, summed_down(): lax.all_to_all(partial_value[None], 'dp', split_axis=2, concat_axis=0, ti...  20.1 us
    all_to_all x1, waiting for transfers between devices, shards(): lax.all_to_all(grad_slots, 'expert', split_axis=0, concat_axis=0, tiled=T...  13.3 us
    broadcast_in_dim x1, local copies, waits for them, and re-layouts, summed_down(): partial_value[None]  12.1 us
  transfers between devices with their start and end apart: 6, of which 4 were waited for; matrix products, arithmetic and copies ran while one was open for 23% of the time, Pallas kernels for 0%

commit v1 on v0

--- a/solution.py
+++ b/solution.py
@@ -28,6 +28,31 @@
 
 
 def shards(tokens, grad_out, expert_ids, gate_q, w_up, w_down):
+
+    def enter_stacks_all_over_axis(incoming_x, axis_no):
+        axis_tag = "dp"
+        main, carry, block_next = (
+            lax.axis_size(axis_tag),
+            lax.axis_index(axis_tag),
+            incoming_x.shape[axis_no],
+        )
+        field_out, block_last = (incoming_x, 1)
+        while block_last < main:
+            field_out = jnp.concatenate(
+                [
+                    field_out,
+                    lax.ppermute(
+                        field_out,
+                        axis_tag,
+                        list(map(lambda idx: (idx, (idx - block_last) % main), range(main))),
+                    ),
+                ],
+                axis=axis_no,
+            )
+            block_last = 2 * block_last
+        near = jnp.roll(field_out, carry * block_next, axis=axis_no)
+        return near
+
     devices = lax.axis_size("expert")
     token_count, top_count = expert_ids.shape
     model_width = tokens.shape[1]
@@ -49,7 +74,7 @@
     grad_slots = empty_rows.at[slot_target].set(slot_grads).reshape(devices, capacity, model_width)
     contract_last = (((1,), (1,)), ((), ()))
     up_whole = lax.all_gather(w_up, "dp", axis=1, tiled=True)[0]
-    down_whole = lax.all_gather(w_down, "dp", axis=2, tiled=True)[0]
+    down_whole = enter_stacks_all_over_axis(w_down, axis_no=2)[0]
     recv_tokens = lax.all_to_all(send_tokens, "expert", split_axis=0, concat_axis=0, tiled=True)
     recv_rows = recv_tokens.reshape(-1, model_width)
     projected = jnp.dot(recv_rows, up_whole, preferred_element_type=jnp.float32)

time: 308 us -> 324 us (1.052)
  waiting for transfers between devices: 114 us -> 120 us
  local copies, waits for them, and re-layouts: 80.2 us -> 85.2 us
  starting transfers between devices: 18.7 us -> 23.5 us
    ppermute x0 -> x2, waiting for transfers between devices: none -> 55 us  [enter_stacks_all_over_axis(): lax.ppermute(field_out, axis_tag, list(map(lambda idx: (idx, (idx - block...]
    all_gather x1 -> x0, waiting for transfers between devices: 34.7 us -> none  [shards(): down_whole = lax.all_gather(w_down, 'dp', axis=2, tiled=True)[0]]
    all_to_all x1, waiting for transfers between devices: 13.3 us -> 0.01 us  [shards(): lax.all_to_all(grad_slots, 'expert', split_axis=0, concat_axis=0, tiled=T...]
    unnamed x15 -> x20, local copies, waits for them, and re-layouts: 24.3 us -> 27.9 us
  transfers between devices with their start and end apart: 6 -> 7, of which waited for: 4 -> 4; matrix products, arithmetic and copies ran while one was open for 23% -> 24% of each run, Pallas kernels for 0% -> 0%
where the time goes in v1:
time: 324 us; the launch traced here: 323 us
  waiting for transfers between devices  120 us (37%)
  local copies, waits for them, and re-layouts  85.2 us (26%)
  other arithmetic  59.8 us (18%)
  starting transfers between devices  23.5 us (7%)
  matrix products  20 us (6%)
  between operations  14.2 us (4%)
    ppermute x2, waiting for transfers between devices, enter_stacks_all_over_axis(): lax.ppermute(field_out, axis_tag, list(map(lambda idx: (idx, (idx - block...  55 us
    unnamed x2, other arithmetic  49.7 us
    all_to_all x1, waiting for transfers between devices, shards(): lax.all_to_all(send_tokens, 'expert', split_axis=0, concat_axis=0, tiled=...  45.8 us
    broadcast_in_dim x1, local copies, waits for them, and re-layouts, summed_up(): partial_value[None]  34 us
    unnamed x20, local copies, waits for them, and re-layouts  27.9 us
    all_to_all x1, waiting for transfers between devices, summed_down(): lax.all_to_all(partial_value[None], 'dp', split_axis=2, concat_axis=0, ti...  18.6 us
    broadcast_in_dim x1, local copies, waits for them, and re-layouts, summed_down(): partial_value[None]  12.1 us
    dot_general x1, matrix products, summed_up(): lax.dot_general(recv_rows, projected_grad, first_dims, preferred_element_...  8.35 us
  transfers between devices with their start and end apart: 7, of which 4 were waited for; matrix products, arithmetic and copies ran while one was open for 24% of the time, Pallas kernels for 0%

profile of v1, /device:TPU:0, one launch (start us, length us, event | category | flops | bytes accessed | tf_op | source)
XLA Modules:
  0.0 322.6 jit_solution(16641994707311124458)
XLA Ops:
  7.2 0.8 copy.25
  8.0 0.1 eq.32
  8.1 0.1 eq.28
  8.2 0.7 broadcast_multiply_fusion
  8.9 1.1 reduce-window.6
  10.0 0.2 slice_reduce_fusion
  10.2 0.1 copy.24
  10.4 0.1 mul.58
  10.5 1.4 broadcast_in_dim.22
  11.9 0.4 reshape.112
  12.3 0.1 fusion.18
  12.4 4.7 %scatter_custom_fusion = bf16[768,1536]{1,0:T(8,128)(2,1)} fusion(s32[512]{0:T(512)S(1)} %bitcast.51, bf16[512,1536]{1,0:T(8,128)(2,1)S(1)} %reshape.112, bf16[]{:T(256)} %constant.36.clone.1), kind=kCustom, calls=%fused_computation.20 | custom fusion | bytes 2359298 | tf_op jit(solution)/shard_map/scatter | solution.py:73
  17.1 0.0 copy-start.1
  17.1 6.5 %all-to-all-start = ((bf16[8,96,1536]{2,1,0:T(8,128)(2,1)}), bf16[8,96,1536]{2,1,0:T(8,128)(2,1)}, u32[]{:S(2)}, u32[]{:S(2)}) async-start(bf16[8,96,1536]{2,1,0:T(8,128)(2,1)} %bitcast.4), calls=%async_computation | async-start | bytes 4718592 | tf_op jit(solution)/shard_map/all_to_all | solution.py:78
  23.6 0.0 copy-done.1
  23.6 0.4 broadcast_in_dim.23
  24.0 0.0 copy-start.2
  24.0 2.3 convert_element_type.78
  26.3 0.0 copy-done.2
  26.3 0.1 copy.27
  26.4 0.1 mul.62
  26.5 6.1 %scatter_custom_fusion.1 = bf16[768,1536]{1,0:T(8,128)(2,1)} fusion(s32[512]{0:T(512)S(1)} %bitcast.52, f32[512,1536]{1,0:T(8,128)} %convert_element_type.78, f32[512]{0:T(512)S(1)} %mul.62, bf16[]{:T(256)} %constant.36.clone.1), kind=kCustom, calls=%fused_computation.15 | custom fusion | flops 1572864 | bytes 5507074 | tf_op jit(solution)/shard_map/scatter | solution.py:74
  32.6 45.8 %all-to-all-done = bf16[8,96,1536]{2,1,0:T(8,128)(2,1)} async-done(((bf16[8,96,1536]{2,1,0:T(8,128)(2,1)}), bf16[8,96,1536]{2,1,0:T(8,128)(2,1)}, u32[]{:S(2)}, u32[]{:S(2)}) %all-to-all-start) | async-done | bytes 2359328 | tf_op jit(solution)/shard_map/all_to_all | solution.py:78
  78.3 0.0 copy-start
  78.3 4.5 %all-to-all-start.1 = ((bf16[8,96,1536]{2,1,0:T(8,128)(2,1)}), bf16[8,96,1536]{2,1,0:T(8,128)(2,1)}, u32[]{:S(2)}, u32[]{:S(2)}) async-start(bf16[8,96,1536]{2,1,0:T(8,128)(2,1)} %bitcast.6), calls=%async_computation.1 | async-start | bytes 4718592 | tf_op jit(solution)/shard_map/all_to_all | solution.py:81
  82.9 0.0 all-gather.2.cloned.1.call-start
  82.9 0.7 all-gather.2.cloned.1.call-update
  83.6 0.0 copy-done
  83.6 2.7 collective-permute-start
  86.3 18.2 %collective-permute-done = bf16[1,768,384]{2,1,0:T(8,128)(2,1)S(1)} collective-permute-done((bf16[1,768,384]{2,1,0:T(8,128)(2,1)S(1)}, bf16[1,768,384]{2,1,0:T(8,128)(2,1)S(1)}, u32[]{:S(2)}, u32[]{:S(2)}) %collective-permute-start) | collective-permute-done | bytes 589856 | tf_op jit(solution)/shard_map/ppermute | solution.py:44
  104.4 0.1 pad_maximum_fusion
  104.5 0.1 collective-permute-start.1
  104.6 1.0 constant_dynamic-update-slice_fusion.5
  105.6 1.0 constant_dynamic-update-slice_fusion.4
  106.6 36.8 %collective-permute-done.1 = bf16[1,768,768]{2,1,0:T(8,128)(2,1)S(1)} collective-permute-done((bf16[1,768,768]{2,1,0:T(8,128)(2,1)S(1)}, bf16[1,768,768]{2,1,0:T(8,128)(2,1)S(1)}, u32[]{:S(2)}, u32[]{:S(2)}) %collective-permute-start.1) | collective-permute-done | bytes 1179680 | tf_op jit(solution)/shard_map/ppermute | solution.py:44
  143.4 1.1 constant_dynamic-update-slice_fusion.3
  144.5 0.9 constant_dynamic-update-slice_fusion.2
  145.5 1.0 constant_dynamic-update-slice_fusion.1
  146.4 1.2 constant_dynamic-update-slice_fusion
  147.6 0.0 all-gather.2.cloned.1.call-done
  147.6 5.8 %fusion.2 = f32[768,768]{1,0:T(8,128)} fusion(bf16[768,1536]{1,0:T(8,128)(2,1)} %bitcast.5, bf16[1,1536,768]{2,1,0:T(8,128)(2,1)} %all-gather.2.cloned.1.call-done), kind=kOutput, calls=%fused_computation.7 | convolution fusion | flops 1811939328 | bytes 7077888 | tf_op jit(solution)/shard_map/dot_general | solution.py:80
  153.4 0.0 all-to-all-done.1
  153.4 8.3 %fusion = bf16[1,1536,768]{2,1,0:T(8,128)(2,1)S(1)} fusion(bf16[768,1536]{1,0:T(8,128)(2,1)} %bitcast.5, f32[768,768]{1,0:T(8,128)} %fusion.2, bf16[768,1536]{1,0:T(8,128)(2,1)} %bitcast.7, bf16[1,768,3072]{2,1,0:T(8,128)(2,1)} %constant_dynamic-update-slice_fusion, s32[]{:T(128)S(6)} %select_n.26), kind=kOutput, calls=%fused_computation.5 | convolution fusion | flops 3630366720 | bytes 11796484 | tf_op jit(solution)/shard_map/dot_general | solution.py:14
  161.7 34.0 %copy.34 = bf16[1,1536,768]{2,0,1:T(2,128)(2,1)} copy(bf16[1,1536,768]{2,1,0:T(8,128)(2,1)S(1)} %fusion) | data formatting | bytes 4718592 | tf_op jit(solution)/shard_map/broadcast_in_dim | solution.py:17
  195.7 0.5 broadcast.72
  196.2 24.1 %reduce.7 = bf16[1536,768]{1,0:T(8,128)(2,1)S(1)} reduce(bf16[1536,1,768]{2,1,0:T(2,128)(2,1)} %bitcast.42, bf16[]{:T(256)} %broadcast.72), dimensions={1}, to_apply=%bitcast.41.reduce_sub_computation | reduce | bytes 4718594
  220.3 2.2 reshape.129
  222.6 5.2 %all-to-all-start.2 = ((bf16[4,2,147456]{2,1,0:T(2,128)(2,1)}), bf16[4,2,147456]{2,1,0:T(2,128)(2,1)S(1)}, u32[]{:S(2)}, u32[]{:S(2)}) async-start(bf16[4,2,147456]{2,1,0:T(2,128)(2,1)} %reshape.129), calls=%async_computation.2 | async-start | bytes 4718592 | tf_op jit(solution)/shard_map/all_to_all | solution.py:17
  227.8 5.8 %fusion.1 = bf16[1,768,1536]{2,1,0:T(8,128)(2,1)} fusion(bf16[768,1536]{1,0:T(8,128)(2,1)} %bitcast.7, f32[768,768]{1,0:T(8,128)} %fusion.2), kind=kOutput, calls=%fused_computation.6 | convolution fusion | flops 1816068096 | bytes 7077888 | tf_op jit(solution)/shard_map/dot_general | solution.py:23
  233.6 12.1 %copy.29 = bf16[1,768,1536]{1,0,2:T(2,128)(2,1)} copy(bf16[1,768,1536]{2,1,0:T(8,128)(2,1)} %fusion.1) | data formatting | bytes 4718592 | tf_op jit(solution)/shard_map/broadcast_in_dim | solution.py:26
  245.7 25.5 %reduce.8 = bf16[1536,768]{1,0:T(8,128)(2,1)} reduce(bf16[1536,1,768]{2,1,0:T(2,128)(2,1)} %bitcast.43, bf16[]{:T(256)} %broadcast.72), dimensions={1}, to_apply=%bitcast.34.reduce_sub_computation | reduce | bytes 4718594
  271.2 4.1 %reshape.131 = bf16[4,2,147456]{2,1,0:T(2,128)(2,1)} reshape(bf16[1536,768]{1,0:T(8,128)(2,1)} %reduce.8) | data formatting | bytes 4718592
  275.4 0.0 all-to-all-done.2
  275.4 4.5 %all-to-all-start.3 = ((bf16[4,2,147456]{2,1,0:T(2,128)(2,1)}), bf16[4,2,147456]{2,1,0:T(2,128)(2,1)}, u32[]{:S(2)}, u32[]{:S(2)}) async-start(bf16[4,2,147456]{2,1,0:T(2,128)(2,1)} %reshape.131), calls=%async_computation.3 | async-start | bytes 4718592 | tf_op jit(solution)/shard_map/all_to_all | solution.py:26
  279.9 3.6 %reshape.130 = bf16[1536,1,768]{2,1,0:T(2,128)(2,1)} reshape(bf16[4,2,147456]{2,1,0:T(2,128)(2,1)S(1)} %all-to-all-done.2) | data formatting | bytes 4718592
  283.4 2.7 copy.31
  286.2 1.3 reduce.4
  287.5 18.6 %all-to-all-done.3 = bf16[4,2,147456]{2,1,0:T(2,128)(2,1)} async-done(((bf16[4,2,147456]{2,1,0:T(2,128)(2,1)}), bf16[4,2,147456]{2,1,0:T(2,128)(2,1)}, u32[]{:S(2)}, u32[]{:S(2)}) %all-to-all-start.3) | async-done | bytes 2359328 | tf_op jit(solution)/shard_map/all_to_all | solution.py:26
  306.1 5.2 %reshape.132 = bf16[1536,1,768]{2,1,0:T(2,128)(2,1)} reshape(bf16[4,2,147456]{2,1,0:T(2,128)(2,1)} %all-to-all-done.3) | data formatting | bytes 4718592
  311.3 2.7 copy.32
  314.0 0.7 reduce_sum.35
  314.7 1.1 copy.30
  (5 shorter events, 0.1 us)
Async XLA Ops:
  17.1 6.5 %copy-start.1 = (bf16[128,1536]{1,0:T(8,128)(2,1)S(1)}, bf16[128,1536]{1,0:T(8,128)(2,1)}, u32[]{:S(2)}) copy-start(bf16[128,1536]{1,0:T(8,128)(2,1)} %param.7) | copy-start | bytes 1179652
  17.1 61.2 %all-to-all-start = ((bf16[8,96,1536]{2,1,0:T(8,128)(2,1)}), bf16[8,96,1536]{2,1,0:T(8,128)(2,1)}, u32[]{:S(2)}, u32[]{:S(2)}) async-start(bf16[8,96,1536]{2,1,0:T(8,128)(2,1)} %bitcast.4), calls=%async_computation | async-start | bytes 4718592 | tf_op jit(solution)/shard_map/all_to_all | solution.py:78
  24.0 2.3 copy-start.2
  78.3 5.2 %copy-start = (bf16[1,768,384]{2,1,0:T(8,128)(2,1)S(1)}, bf16[1,768,384]{2,1,0:T(8,128)(2,1)}, u32[]{:S(2)}) copy-start(bf16[1,768,384]{2,1,0:T(8,128)(2,1)} %param.11) | copy-start | bytes 1769476
  78.3 75.0 %all-to-all-start.1 = ((bf16[8,96,1536]{2,1,0:T(8,128)(2,1)}), bf16[8,96,1536]{2,1,0:T(8,128)(2,1)}, u32[]{:S(2)}, u32[]{:S(2)}) async-start(bf16[8,96,1536]{2,1,0:T(8,128)(2,1)} %bitcast.6), calls=%async_computation.1 | async-start | bytes 4718592 | tf_op jit(solution)/shard_map/all_to_all | solution.py:81
  82.9 64.7 %all-gather.2.cloned.1.call-start = ((), (), s32[]{:S(2)}) async-start(), calls=%async_computation.4 | async-start | bytes 2949120 | tf_op jit(solution)/shard_map/all_gather | solution.py:76
  83.6 20.8 %collective-permute-start = (bf16[1,768,384]{2,1,0:T(8,128)(2,1)S(1)}, bf16[1,768,384]{2,1,0:T(8,128)(2,1)S(1)}, u32[]{:S(2)}, u32[]{:S(2)}) collective-permute-start(bf16[1,768,384]{2,1,0:T(8,128)(2,1)S(1)} %copy-done), channel_id=1, source_target_pairs={{0,24},{8,0},{16,8},{24,16},{1,25},{9,1},{17,9},{25,17},{2,26},{10... | collective-permute-start | bytes 1769480 | tf_op jit(solution)/shard_map/ppermute | solution.py:44
  104.5 38.9 %collective-permute-start.1 = (bf16[1,768,768]{2,1,0:T(8,128)(2,1)S(1)}, bf16[1,768,768]{2,1,0:T(8,128)(2,1)S(1)}, u32[]{:S(2)}, u32[]{:S(2)}) collective-permute-start(bf16[1,768,768]{2,1,0:T(8,128)(2,1)S(1)} %pad_maximum_fusion), channel_id=1, source_target_pairs={{0,16},{8,24},{16,0},{24,8},{1,17},{9,25},{17,1},{25,9},{2,18},{10... | collective-permute-start | bytes 3538952 | tf_op jit(solution)/shard_map/ppermute | solution.py:44
  222.6 52.8 %all-to-all-start.2 = ((bf16[4,2,147456]{2,1,0:T(2,128)(2,1)}), bf16[4,2,147456]{2,1,0:T(2,128)(2,1)S(1)}, u32[]{:S(2)}, u32[]{:S(2)}) async-start(bf16[4,2,147456]{2,1,0:T(2,128)(2,1)} %reshape.129), calls=%async_computation.2 | async-start | bytes 4718592 | tf_op jit(solution)/shard_map/all_to_all | solution.py:17
  275.4 30.7 %all-to-all-start.3 = ((bf16[4,2,147456]{2,1,0:T(2,128)(2,1)}), bf16[4,2,147456]{2,1,0:T(2,128)(2,1)}, u32[]{:S(2)}, u32[]{:S(2)}) async-start(bf16[4,2,147456]{2,1,0:T(2,128)(2,1)} %reshape.131), calls=%async_computation.3 | async-start | bytes 4718592 | tf_op jit(solution)/shard_map/all_to_all | solution.py:26
Sparse Core Ops, SparseCore 0:
  85.5 55.7 all-gather.1
